TPU v7x, 32 devices: a whole 2x2x4 slice. The times are simulated.
32 devices in a mesh: dp: 8 (over z, y), tensor: 4 (over x, core).
Axes of the slice: x: 2, y: 2, z: 4, core: 2. Of those that a mesh axis runs over, the one named last changes fastest.
Arguments:
- activations: bfloat16 [2048, 8192], P('dp'), may hold values from -6 to 6
- key_value_grads: bfloat16 [2048, 2, 1024], P('dp', None, 'tensor'), may hold values from -6 to 6
- owner_table: int32 [64], replicated, may hold values from 0 to 63, each once
- left_factors: float32 [4, 64, 512, 512], P('tensor', 'dp'), may hold values from -16 to 16, as said below
- right_factors: float32 [4, 64, 128, 128], P('tensor', 'dp'), may hold values from -16 to 16, as said below
Outputs:
- left_updated: float32 [4, 64, 512, 512], P('tensor', 'dp')
- right_updated: float32 [4, 64, 128, 128], P('tensor', 'dp')
- update: bfloat16 [2, 8192, 1024], P(None, 'dp')
Inputs may be any that keep to these rules, and one draw needn't show every extreme that they name: `owner_table`: each block number appears once; slot s lies on index s // 8 of dp. `left_factors`: every block is symmetric positive definite. `right_factors`: every block is symmetric positive definite.
All inputs are finite; a program needn't handle non-finite values.
Results may differ from a plain program's by a relative error of at most 0.012.
The roundings to bfloat16 on the way count: a program that leaves them out, or rounds other values in their place, can miss the bound.
Values may be sent and summed in bfloat16 or wider, within the bound.
A program may use at most 128 MiB of HBM per device.

v0:
```python
import jax
import jax.numpy as jnp
from jax import lax
from jax.sharding import PartitionSpec as P

ITERS = 8


MOMENT_DECAY = 0.9
RIDGE_SHARE = 0.0001
EXACT_MODE = lax.Precision.HIGHEST


def for_sending(x):

    def short(part):
        return part.astype(jnp.bfloat16) if part.dtype == jnp.float32 else part

    return jax.tree.map(short, x)


def product(left_mat, right_mat):
    return jnp.dot(left_mat, right_mat, precision=EXACT_MODE, preferred_element_type=jnp.float32)


def coarse_product(left_mat, right_mat):
    return jnp.dot(
        left_mat.astype(jnp.bfloat16),
        right_mat.astype(jnp.bfloat16),
        preferred_element_type=jnp.float32,
    )


def inverse_root(matrix):
    order_dim = matrix.shape[0]
    identity_mat = jnp.eye(order_dim, dtype=jnp.float32)
    shifted = matrix + RIDGE_SHARE * jnp.trace(matrix) / order_dim * identity_mat
    scaling = 2.5 / jnp.sqrt(jnp.sum(shifted * shifted))
    result = jnp.sqrt(jnp.sqrt(scaling)) * identity_mat
    powered = scaling * shifted
    for iteration in range(ITERS):
        factor = (5.0 * identity_mat - powered) * 0.25
        result = coarse_product(result, factor)
        if iteration + 1 < ITERS:
            squared = coarse_product(factor, factor)
            powered = coarse_product(coarse_product(squared, squared), powered)
    return result


def block_step(inputs):
    gradient, left_old, right_old = inputs
    left_new = MOMENT_DECAY * left_old + (1.0 - MOMENT_DECAY) * product(gradient, gradient.T)
    right_new = MOMENT_DECAY * right_old + (1.0 - MOMENT_DECAY) * product(gradient.T, gradient)
    precond = product(product(inverse_root(left_new), gradient), inverse_root(right_new))
    direction = precond / jnp.sqrt(jnp.mean(precond * precond) + 1e-06)
    return (left_new, right_new, direction.astype(jnp.bfloat16))


def landing(slot_ids, owner_table, block_order, piece_rows, shard_rows, row_blocks, col_blocks):
    block_ids = jnp.take(owner_table, slot_ids)
    per_projection = row_blocks * col_blocks
    projection = block_ids // per_projection
    remainder = block_ids % per_projection
    row_block = remainder // col_blocks
    column = remainder % col_blocks
    per_block = block_order // piece_rows
    pieces = row_block[:, None] * per_block + jnp.arange(per_block, dtype=jnp.int32)[None, :]
    per_shard = shard_rows // piece_rows
    return (projection, column, pieces // per_shard, pieces % per_shard)


def to_mine(projection, column, target, local_pos, position, per_shard, col_blocks):
    landing_hits = (target == position)[:, :, None, None, None]
    landing_hits = landing_hits & (
        projection[:, None, None, None, None]
        == jnp.arange(2, dtype=jnp.int32)[None, None, :, None, None]
    )
    landing_hits = landing_hits & (
        local_pos[:, :, None, None, None]
        == jnp.arange(per_shard, dtype=jnp.int32)[None, None, None, :, None]
    )
    landing_hits = landing_hits & (
        column[:, None, None, None, None]
        == jnp.arange(col_blocks, dtype=jnp.int32)[None, None, None, None, :]
    )
    return landing_hits.astype(jnp.bfloat16)


def regroup(blocks_data, owner_table, shard_rows, row_blocks, col_blocks, shards):
    slot_count, block_order, width = blocks_data.shape
    cols_block = width // shards
    piece_rows = min(shard_rows, block_order)
    per_block = block_order // piece_rows
    per_shard = shard_rows // piece_rows
    position = lax.axis_index("dp")
    initial = jnp.zeros((2, per_shard, piece_rows, shards, col_blocks, cols_block), jnp.float32)
    shard_part = jax.tree.map(
        lambda part: lax.all_gather(part, "dp", axis=0, tiled=True), for_sending(blocks_data)
    )
    count_here = shard_part.shape[0]
    slot_ids = jnp.arange(count_here, dtype=jnp.int32)
    projection, column, target, local_pos = landing(
        slot_ids, owner_table, block_order, piece_rows, shard_rows, row_blocks, col_blocks
    )
    landing_hits = to_mine(projection, column, target, local_pos, position, per_shard, col_blocks)
    assembled = initial + jnp.einsum(
        "smjpc,smqtk->jpqtck",
        landing_hits,
        shard_part.reshape(count_here, per_block, piece_rows, shards, cols_block),
        preferred_element_type=jnp.float32,
    )
    return assembled.astype(jnp.bfloat16).reshape(2, shard_rows, shards * col_blocks * cols_block)


def local(activations, key_value_grads, owner_table, left_factors, right_factors):
    rows_block = left_factors.shape[2]
    cols_block = right_factors.shape[2]
    rank_count = lax.axis_size("dp")
    row_blocks = activations.shape[1] // rows_block
    col_blocks = key_value_grads.shape[2] // cols_block
    per_projection = row_blocks * col_blocks
    shard_rows = activations.shape[1] // rank_count
    inverse_tokens = 1.0 / (activations.shape[0] * rank_count)

    def one_block(block_id):
        projection = block_id // per_projection
        remainder = block_id % per_projection
        row_start = remainder // col_blocks * rows_block
        col_start = remainder % col_blocks * cols_block
        left_part = lax.dynamic_slice_in_dim(activations, row_start, rows_block, 1)
        chosen = lax.dynamic_index_in_dim(key_value_grads, projection, 1, keepdims=False)
        right_part = lax.dynamic_slice_in_dim(chosen, col_start, cols_block, 1)
        summed = lax.dot_general(
            left_part, right_part, (((0,), (0,)), ((), ())), preferred_element_type=jnp.float32
        )
        return summed * inverse_tokens

    gradients = lax.psum_scatter(
        lax.map(one_block, owner_table), "dp", scatter_dimension=0, tiled=True
    )
    left_new, right_new, directions = lax.map(
        block_step, (gradients, left_factors[0], right_factors[0])
    )
    own_rows = regroup(directions, owner_table, shard_rows, row_blocks, col_blocks, 1)
    update = lax.all_gather(own_rows, "tensor", axis=2, tiled=True)
    return (left_new[None], right_new[None], update)


def solution(mesh):
    in_specs = (
        P("dp", None),
        P("dp", None, "tensor"),
        P(),
        P("tensor", "dp", None, None),
        P("tensor", "dp", None, None),
    )
    out_specs = (P("tensor", "dp", None, None), P("tensor", "dp", None, None), P(None, "dp", None))
    return jax.shard_map(local, mesh=mesh, in_specs=in_specs, out_specs=out_specs, check_vma=False)
```

profile of v0, /device:TPU:0, one launch (start us, length us, event | category | flops | bytes accessed | tf_op | source)
XLA Modules:
  0.0 1126.5 jit_solution(6807661372749703518)
XLA Ops:
  8.2 376.1 %while.29 = (s32[]{:T(128)}, f32[64,512,128]{2,1,0:T(8,128)}, s32[64]{0:T(128)}, bf16[256,8192]{1,0:T(8,128)(2,1)}, bf16[256,2,256]{2,0,1:T(8,128)(2,1)S(1)}, /*...) while((s32[]{:T(128)}, f32[64,512,128]{2,1,0:T(8,128)}, ...), condition=%wide.region_1.2_spmd, body=%wide.region_0.1_spmd.sunk | while | flops 33620020 | bytes 591041 | solution.py:139
  59.1 2.0 fusion.384
  76.7 2.0 fusion.384
  141.3 2.0 fusion.384
  164.9 2.0 fusion.384
  200.1 2.0 fusion.384
  247.2 2.0 fusion.384
  253.1 2.0 fusion.384
  347.0 2.0 fusion.384
  384.4 283.0 %reduce-scatter.2.cloned.1.call-done = f32[8,512,128]{2,1,0:T(8,128)} async-done(((f32[64,512,128]{2,1,0:T(8,128)}), f32[8,512,128]{2,1,0:T(8,128)}) %reduce-scatter.2.cloned.1.call-update) | async-done | bytes 2097168 | tf_op jit(solution)/shard_map/reduce_scatter | solution.py:138
  667.3 280.6 %while.30 = (s32[]{:T(128)}, f32[8,512,512]{2,1,0:T(8,128)}, f32[8,128,128]{2,1,0:T(8,128)}, bf16[8,512,128]{2,1,0:T(8,128)(2,1)}, f32[8,512,512]{2,1,0:T(8,128)...) while((s32[]{:T(128)}, f32[8,512,512]{2,1,0:T(8,128)}, ...), condition=%wide.region_9.10_spmd, body=%wide.region_3.9_spmd.sunk | while | flops 8948252672 | bytes 52104520 | solution.py:141
  667.3 2.3 bitcast_dynamic-update-slice_fusion.7
  676.2 3.5 bitcast_dynamic-update-slice_fusion.6
  702.4 2.3 bitcast_dynamic-update-slice_fusion.7
  711.2 3.5 bitcast_dynamic-update-slice_fusion.6
  737.5 2.3 bitcast_dynamic-update-slice_fusion.7
  746.3 3.5 bitcast_dynamic-update-slice_fusion.6
  772.6 2.3 bitcast_dynamic-update-slice_fusion.7
  781.4 3.5 bitcast_dynamic-update-slice_fusion.6
  807.6 2.3 bitcast_dynamic-update-slice_fusion.7
  816.5 3.5 bitcast_dynamic-update-slice_fusion.6
  842.8 2.3 bitcast_dynamic-update-slice_fusion.7
  851.6 3.5 bitcast_dynamic-update-slice_fusion.6
  877.9 2.3 bitcast_dynamic-update-slice_fusion.7
  886.7 3.5 bitcast_dynamic-update-slice_fusion.6
  912.9 2.3 bitcast_dynamic-update-slice_fusion.7
  921.7 3.5 bitcast_dynamic-update-slice_fusion.6
  948.0 3.0 copy.10
  952.0 123.2 %all-gather.3.cloned.1.call-done = bf16[64,512,128]{2,0,1:T(8,128)(2,1)} async-done(((bf16[8,512,128]{2,0,1:T(8,128)(2,1)}), bf16[64,512,128]{2,0,1:T(8,128)(2,1)}) %all-gather.3.cloned.1.call-update) | async-done | bytes 8388624 | tf_op jit(solution)/shard_map/all_gather | solution.py:98
  1075.2 4.6 fusion.263
  1082.0 33.3 %all-gather.5.cloned.1.call-done = bf16[2,1024,1024]{2,1,0:T(8,128)(2,1)} async-done(((bf16[2,1024,256]{2,1,0:T(8,128)(2,1)}), bf16[2,1024,1024]{2,1,0:T(8,128)(2,1)}) %all-gather.5.cloned.1.call-update) | async-done | bytes 4194320 | tf_op jit(solution)/shard_map/all_gather | solution.py:145
  1115.4 4.6 copy.38
  (489 shorter events, 402.6 us)
Async XLA Ops:
  7.2 660.2 %reduce-scatter.2.cloned.1.call-start = ((), (), s32[]{:S(2)}) async-start(), calls=%async_computation.1 | async-start | bytes 18874368 | tf_op jit(solution)/shard_map/reduce_scatter | solution.py:138
  384.3 690.9 %all-gather.3.cloned.1.call-start = ((), (), s32[]{:S(2)}) async-start(), calls=%async_computation.2 | async-start | bytes 9437184 | tf_op jit(solution)/shard_map/all_gather | solution.py:98
  667.3 283.7 %copy-start = (s32[64]{0:T(128)S(1)}, s32[64]{0:T(128)}, u32[]{:S(2)}) copy-start(s32[64]{0:T(128)} %get-tuple-element.428) | copy-start | bytes 772
  951.0 164.4 %all-gather.5.cloned.1.call-start = ((), (), s32[]{:S(2)}) async-start(), calls=%async_computation.3 | async-start | bytes 5242880 | tf_op jit(solution)/shard_map/all_gather | solution.py:145
Sparse Core Ops, SparseCore 0:
  384.4 282.8 reduce-scatter.1
  951.1 124.0 all-gather.2
  1082.1 33.1 all-gather.4
where the time goes:
time: 1130 us
  waiting for transfers between devices  440 us (39%)
  matrix products  358 us (32%)
  loops' own time  196 us (17%)
  local copies, waits for them, and re-layouts  90.7 us (8%)
  other arithmetic  27.6 us (2%)
  between operations  13.9 us (1%)
    reduce_scatter x1, waiting for transfers between devices, local(): lax.psum_scatter(lax.map(one_block, owner_table), 'dp', scatter_dimension...  283 us
    another operation x1, loops' own time, local(): lax.map(one_block, owner_table)  170 us
    dot_general x288, matrix products, coarse_product(): jnp.dot(left_mat.astype(jnp.bfloat16), right_mat.astype(jnp.bfloat16), pr...  158 us
    dot_general x64, matrix products, one_block(): lax.dot_general(left_part, right_part, (((0,), (0,)), ((), ())), preferre...  127 us
    all_gather x1, waiting for transfers between devices, regroup(): lax.all_gather(part, 'dp', axis=0, tiled=True)  123 us
    dynamic_slice x64, local copies, waits for them, and re-layouts, local(): lax.map(one_block, owner_table)  79.2 us
    dot_general x32, matrix products, product(): jnp.dot(left_mat, right_mat, precision=EXACT_MODE, preferred_element_type...  69.1 us
    all_gather x1, waiting for transfers between devices, local(): update = lax.all_gather(own_rows, 'tensor', axis=2, tiled=True)  33.3 us
  transfers between devices with their start and end apart: 3, of which 3 were waited for; matrix products, arithmetic and copies ran while one was open for 0% of the time, Pallas kernels for 0%

commit v1 on v0

v1 whole, which is shorter than its diff:
```python
import functools

import jax
import jax.numpy as jnp
from jax import lax
from jax.experimental import pallas as pl
from jax.experimental.pallas import tpu as pltpu
from jax.sharding import PartitionSpec as P

ITERS = 8
MOMENT_DECAY = 0.9
RIDGE_SHARE = 0.0001
CHUNK_SLOTS = 2
VMEM_LIMIT = 60 * 1024 * 1024


def dot(left_mat, right_mat):
    return jnp.dot(left_mat, right_mat, preferred_element_type=jnp.float32)


def halves(x):
    high = x.astype(jnp.bfloat16)
    low = (x - high.astype(jnp.float32)).astype(jnp.bfloat16)
    return high, low


def gradient_kernel(
    table_ref, act_ref, kv_ref, out_ref, *, chunk, chunk_slots, slots, per_projection, col_blocks, scale
):
    rows_block, cols_block = out_ref.shape[2:]
    width = col_blocks * cols_block
    first = pl.program_id(0) * slots + chunk * chunk_slots
    for k in range(chunk_slots):
        block_id = table_ref[first + k]
        projection = block_id // per_projection
        remainder = block_id % per_projection
        row_start = pl.multiple_of(remainder // col_blocks * rows_block, rows_block)
        col_start = pl.multiple_of(
            projection * width + remainder % col_blocks * cols_block, cols_block
        )
        summed = lax.dot_general(
            act_ref[:, pl.ds(row_start, rows_block)],
            kv_ref[:, pl.ds(col_start, cols_block)],
            (((0,), (0,)), ((), ())),
            preferred_element_type=jnp.float32,
        )
        out_ref[0, k] = summed * scale


def gradient_chunk(table, activations, cotangents, chunk, chunk_slots, ranks, rows_block, cols_block, col_blocks):
    tokens, model = activations.shape
    slots = table.shape[0] // ranks
    body = functools.partial(
        gradient_kernel,
        chunk=chunk,
        chunk_slots=chunk_slots,
        slots=slots,
        per_projection=model // rows_block * col_blocks,
        col_blocks=col_blocks,
        scale=1.0 / (tokens * ranks),
    )
    return pl.pallas_call(
        body,
        out_shape=jax.ShapeDtypeStruct((ranks, chunk_slots, rows_block, cols_block), jnp.float32),
        grid_spec=pltpu.PrefetchScalarGridSpec(
            num_scalar_prefetch=1,
            grid=(ranks,),
            in_specs=[
                pl.BlockSpec(activations.shape, lambda d, t: (0, 0), pipeline_mode=pl.Buffered(1)),
                pl.BlockSpec(cotangents.shape, lambda d, t: (0, 0), pipeline_mode=pl.Buffered(1)),
            ],
            out_specs=pl.BlockSpec(
                (1, chunk_slots, rows_block, cols_block), lambda d, t: (d, 0, 0, 0)
            ),
        ),
        compiler_params=pltpu.CompilerParams(vmem_limit_bytes=VMEM_LIMIT),
        cost_estimate=pl.CostEstimate(
            flops=2 * ranks * chunk_slots * rows_block * cols_block * tokens,
            bytes_accessed=activations.size * 2 + ranks * chunk_slots * rows_block * cols_block * 4,
            transcendentals=0,
        ),
    )(table, activations, cotangents)


def diagonal(order):
    rows = lax.broadcasted_iota(jnp.int32, (order, order), 0)
    return rows == lax.broadcasted_iota(jnp.int32, (order, order), 1)


def total(x):
    return jnp.sum(jnp.sum(x, axis=1, keepdims=True), axis=0, keepdims=True)


def factor_of(powered, on_diagonal):
    return ((jnp.where(on_diagonal, 5.0, 0.0) - powered) * 0.25).astype(jnp.bfloat16)


def begin_root(updated, m_ref, f_ref, x_ref):
    order = updated.shape[0]
    on_diagonal = diagonal(order)
    trace = total(jnp.where(on_diagonal, updated, 0.0))
    shifted = updated + jnp.where(on_diagonal, RIDGE_SHARE * trace / order, 0.0)
    scaling = 2.5 / jnp.sqrt(total(shifted * shifted))
    powered = scaling * shifted
    factor = factor_of(powered, on_diagonal)
    start = jnp.sqrt(jnp.sqrt(scaling)).astype(jnp.bfloat16).astype(jnp.float32)
    m_ref[...] = powered.astype(jnp.bfloat16)
    f_ref[...] = factor
    x_ref[...] = start * factor.astype(jnp.float32)


def root_steps(groups):
    squares = []
    for m_ref, f_ref, x_ref in groups:
        factor = f_ref[...]
        squares.append(dot(factor, factor).astype(jnp.bfloat16))
    fourths = [dot(s, s).astype(jnp.bfloat16) for s in squares]
    for fourth, (m_ref, f_ref, x_ref) in zip(fourths, groups):
        powered = dot(fourth, m_ref[...])
        m_ref[...] = powered.astype(jnp.bfloat16)
        f_ref[...] = factor_of(powered, diagonal(powered.shape[0]))
    for m_ref, f_ref, x_ref in groups:
        x_ref[...] = dot(x_ref[...].astype(jnp.bfloat16), f_ref[...])


def block_kernel(grad_ref, left_ref, right_ref, *rest, chunk_slots, chained):
    if chained:
        rest = rest[2:]
    left_out, right_out, dir_ref, ml, fl, xl, mr, fr, xr = rest
    groups = []
    for k in range(chunk_slots):
        grad = grad_ref[k]
        high, low = halves(grad)
        flipped = grad.T
        high_t, low_t = halves(flipped)
        wide = jnp.concatenate([high, high, low], axis=1)
        wide_t = jnp.concatenate([high_t, high_t, low_t], axis=1)
        tall = jnp.concatenate([high, low, high], axis=0)
        tall_t = jnp.concatenate([high_t, low_t, high_t], axis=0)
        left_new = MOMENT_DECAY * left_ref[k] + (1.0 - MOMENT_DECAY) * dot(wide, tall_t)
        right_new = MOMENT_DECAY * right_ref[k] + (1.0 - MOMENT_DECAY) * dot(wide_t, tall)
        left_out[k] = left_new
        right_out[k] = right_new
        begin_root(left_new, ml.at[k], fl.at[k], xl.at[k])
        begin_root(right_new, mr.at[k], fr.at[k], xr.at[k])
        groups.append((ml.at[k], fl.at[k], xl.at[k]))
        groups.append((mr.at[k], fr.at[k], xr.at[k]))

    def step(_, carry):
        root_steps(groups)
        return carry

    lax.fori_loop(0, ITERS - 1, step, 0)
    for k in range(chunk_slots):
        high, low = halves(grad_ref[k])
        tall = jnp.concatenate([high, low, high], axis=0)
        root_high, root_low = halves(xl[k])
        half = dot(jnp.concatenate([root_high, root_high, root_low], axis=1), tall)
        half_high, half_low = halves(half)
        right_high, right_low = halves(xr[k])
        precond = dot(
            jnp.concatenate([half_high, half_high, half_low], axis=1),
            jnp.concatenate([right_high, right_low, right_high], axis=0),
        )
        mean = total(precond * precond) / precond.size
        dir_ref[k] = (precond / jnp.sqrt(mean + 1e-06)).astype(jnp.bfloat16)


def block_chunk(grads, left_factors, right_factors, chunk, before):
    chunk_slots, rows_block, cols_block = grads.shape

    def pick(*tail):
        return pl.BlockSpec((chunk_slots,) + tail, lambda g: (chunk, 0, 0))

    def whole(*tail):
        return pl.BlockSpec((chunk_slots,) + tail, lambda g: (0, 0, 0))

    chained = before is not None
    specs = [
        whole(rows_block, cols_block),
        pick(rows_block, rows_block),
        pick(cols_block, cols_block),
    ]
    operands = [grads, left_factors, right_factors]
    aliases = {}
    if chained:
        specs += [pl.BlockSpec(memory_space=pl.ANY)] * 2
        operands += list(before)
        aliases = {3: 0, 4: 1}

    def scratch(order):
        square = (chunk_slots, order, order)
        return [
            pltpu.VMEM(square, jnp.bfloat16),
            pltpu.VMEM(square, jnp.bfloat16),
            pltpu.VMEM(square, jnp.float32),
        ]

    return pl.pallas_call(
        functools.partial(block_kernel, chunk_slots=chunk_slots, chained=chained),
        grid=(1,),
        out_shape=(
            jax.ShapeDtypeStruct(left_factors.shape, jnp.float32),
            jax.ShapeDtypeStruct(right_factors.shape, jnp.float32),
            jax.ShapeDtypeStruct(grads.shape, jnp.bfloat16),
        ),
        in_specs=specs,
        out_specs=(
            pick(rows_block, rows_block),
            pick(cols_block, cols_block),
            whole(rows_block, cols_block),
        ),
        scratch_shapes=scratch(rows_block) + scratch(cols_block),
        input_output_aliases=aliases,
        compiler_params=pltpu.CompilerParams(vmem_limit_bytes=VMEM_LIMIT),
        cost_estimate=pl.CostEstimate(
            flops=2 * chunk_slots * rows_block**3 * 4 * ITERS,
            bytes_accessed=chunk_slots * rows_block * rows_block * 8,
            transcendentals=0,
        ),
    )(*operands)


def pick_kernel(dev_ref, pos_ref, sub_ref, *refs, shape, chunk_slots, piece_rows, cols_block):
    sources, out_ref, sem = refs[:-2], refs[-2], refs[-1]
    projections, per_shard, col_blocks = shape
    index = 0
    for projection in range(projections):
        for piece in range(per_shard):
            for column in range(col_blocks):
                dest = out_ref.at[
                    projection,
                    pl.ds(piece * piece_rows, piece_rows),
                    pl.ds(column * cols_block, cols_block),
                ]
                rows = pl.ds(pl.multiple_of(sub_ref[piece] * piece_rows, piece_rows), piece_rows)
                for chunk, source in enumerate(sources):

                    @pl.when(pos_ref[index] // chunk_slots == chunk)
                    def _():
                        pltpu.make_async_copy(
                            source.at[dev_ref[index], pos_ref[index] % chunk_slots, rows], dest, sem.at[index]
                        ).start()

                index += 1
    index = 0
    for projection in range(projections):
        for piece in range(per_shard):
            for column in range(col_blocks):
                dest = out_ref.at[
                    projection,
                    pl.ds(piece * piece_rows, piece_rows),
                    pl.ds(column * cols_block, cols_block),
                ]
                pltpu.make_async_copy(
                    sources[0].at[0, 0, pl.ds(0, piece_rows)], dest, sem.at[index]
                ).wait()
                index += 1


def pick_rows(gathered, owner_table, shard_rows, row_blocks, col_blocks, slots):
    _, chunk_slots, block_order, cols_block = gathered[0].shape
    piece_rows = min(shard_rows, block_order)
    per_block = block_order // piece_rows
    per_shard = shard_rows // piece_rows
    pieces = lax.axis_index("dp") * per_shard + jnp.arange(per_shard, dtype=jnp.int32)
    wanted = (
        jnp.arange(2, dtype=jnp.int32)[:, None, None] * row_blocks + (pieces // per_block)[None, :, None]
    ) * col_blocks + jnp.arange(col_blocks, dtype=jnp.int32)[None, None, :]
    hits = wanted.reshape(-1)[:, None] == owner_table[None, :]
    where = jnp.sum(
        jnp.where(hits, jnp.arange(owner_table.shape[0], dtype=jnp.int32)[None, :], 0), axis=1, dtype=jnp.int32
    )
    count = 2 * per_shard * col_blocks
    body = functools.partial(
        pick_kernel,
        shape=(2, per_shard, col_blocks),
        chunk_slots=chunk_slots,
        piece_rows=piece_rows,
        cols_block=cols_block,
    )
    shape = (2, shard_rows, col_blocks * cols_block)
    return pl.pallas_call(
        body,
        out_shape=jax.ShapeDtypeStruct(shape, jnp.bfloat16),
        grid_spec=pltpu.PrefetchScalarGridSpec(
            num_scalar_prefetch=3,
            grid=(1,),
            in_specs=[pl.BlockSpec(memory_space=pl.ANY)] * len(gathered),
            out_specs=pl.BlockSpec(shape, lambda g, *_: (0, 0, 0)),
            scratch_shapes=[pltpu.SemaphoreType.DMA((count,))],
        ),
    )(where // slots, where % slots, pieces % per_block, *gathered)


def local(activations, key_value_grads, owner_table, left_factors, right_factors):
    rows_block = left_factors.shape[2]
    cols_block = right_factors.shape[2]
    ranks = lax.axis_size("dp")
    row_blocks = activations.shape[1] // rows_block
    col_blocks = key_value_grads.shape[2] // cols_block
    shard_rows = activations.shape[1] // ranks
    slots = left_factors.shape[1]
    chunk_slots = min(CHUNK_SLOTS, slots)
    cotangents = key_value_grads.reshape(key_value_grads.shape[0], -1)
    grads = []
    for chunk in range(slots // chunk_slots):
        partial = gradient_chunk(
            owner_table, activations, cotangents, chunk, chunk_slots, ranks, rows_block, cols_block, col_blocks
        )
        grads.append(lax.psum_scatter(partial, "dp", scatter_dimension=0, tiled=True)[0])
    before = None
    gathered = []
    for chunk, grad in enumerate(grads):
        left_new, right_new, directions = block_chunk(grad, left_factors[0], right_factors[0], chunk, before)
        before = (left_new, right_new)
        gathered.append(lax.all_gather(directions, "dp", axis=0))
    own_rows = pick_rows(gathered, owner_table, shard_rows, row_blocks, col_blocks, slots)
    update = lax.all_gather(own_rows, "tensor", axis=2, tiled=True)
    return (left_new[None], right_new[None], update)


def solution(mesh):
    in_specs = (
        P("dp", None),
        P("dp", None, "tensor"),
        P(),
        P("tensor", "dp", None, None),
        P("tensor", "dp", None, None),
    )
    out_specs = (P("tensor", "dp", None, None), P("tensor", "dp", None, None), P(None, "dp", None))
    return jax.shard_map(local, mesh=mesh, in_specs=in_specs, out_specs=out_specs, check_vma=False)
```

time: 1130 us -> 655 us (0.58)
  matrix products: 358 us -> 0 us
  loops' own time: 196 us -> 0 us
  Pallas kernels: 0 us -> 133 us
  local copies, waits for them, and re-layouts: 90.7 us -> 6.99 us
  waiting for transfers between devices: 440 us -> 499 us
  other arithmetic: 27.6 us -> 0.93 us
    dot_general x385 -> x0, matrix products: 358 us -> none  [the longest x288 158 us: coarse_product(): jnp.dot(left_mat.astype(jnp.bfloat16), right_mat.astype(jnp.bfloat16), pr...]
    another operation x2 -> x0, loops' own time: 196 us -> none  [the longest x1 170 us: local(): lax.map(one_block, owner_table)]
    pallas_call x0 -> x9, Pallas kernels: none -> 133 us  [the longest x4 97.6 us: block_chunk(): pl.pallas_call(functools.partial(block_kernel, chunk_slots=chunk_slots, c...]
    dynamic_slice x64 -> x0, local copies, waits for them, and re-layouts: 79.2 us -> none  [local(): lax.map(one_block, owner_table)]
    all_gather x1 -> x4, waiting for transfers between devices: 123 us -> 195 us  [local(): gathered.append(lax.all_gather(directions, 'dp', axis=0))]
    reduce_sum x32 -> x1, other arithmetic: 22 us -> 0.18 us  [pick_rows(): jnp.sum(jnp.where(hits, jnp.arange(owner_table.shape[0], dtype=jnp.int32)...]
    reduce_scatter x1 -> x4, waiting for transfers between devices: 283 us -> 268 us  [local(): lax.psum_scatter(partial, 'dp', scatter_dimension=0, tiled=True)[0]]
  transfers between devices with their start and end apart: 3 -> 9, of which waited for: 3 -> 9; matrix products, arithmetic and copies ran while one was open for 0% -> 0% of each run, Pallas kernels for 0% -> 15%
where the time goes in v1:
time: 655 us; the launch traced here: 654 us
  waiting for transfers between devices  499 us (76%)
  Pallas kernels  133 us (20%)
  between operations  13.9 us (2%)
  local copies, waits for them, and re-layouts  6.99 us (1%)
    reduce_scatter x4, waiting for transfers between devices, local(): lax.psum_scatter(partial, 'dp', scatter_dimension=0, tiled=True)[0]  268 us
    all_gather x4, waiting for transfers between devices, local(): gathered.append(lax.all_gather(directions, 'dp', axis=0))  195 us
    pallas_call x4, Pallas kernels, block_chunk(): pl.pallas_call(functools.partial(block_kernel, chunk_slots=chunk_slots, c...  97.6 us
    all_gather x1, waiting for transfers between devices, local(): update = lax.all_gather(own_rows, 'tensor', axis=2, tiled=True)  33.7 us
    pallas_call x4, Pallas kernels, gradient_chunk(): pl.pallas_call(body, out_shape=jax.ShapeDtypeStruct((ranks, chunk_slots,...  32.8 us
  transfers between devices with their start and end apart: 9, of which 9 were waited for; matrix products, arithmetic and copies ran while one was open for 0% of the time, Pallas kernels for 15%

profile of v1, /device:TPU:0, one launch (start us, length us, event | category | flops | bytes accessed | tf_op | source)
XLA Modules:
  0.0 654.3 jit_solution(9552812316786612481)
XLA Ops:
  7.2 1.7 copy.14
  8.9 8.0 %shard_map.79 = f32[8,2,512,128]{3,2,1,0:T(8,128)} custom-call(s32[64]{0:T(128)} %table_ref.7, bf16[256,8192]{1,0:T(8,128)(2,1)} %act_ref.7, bf16[256,512]{1,0:T(8,128)(2,1)} %bitcast.14), custom_call_target="tpu_custom_call" | custom-call | flops 536870912 | bytes 8388608 | tf_op jit(solution)/shard_map/pallas_call | solution.py:62
  16.9 0.0 reduce-scatter.9.cloned.1.call-start
  17.0 8.2 %shard_map.78 = f32[8,2,512,128]{3,2,1,0:T(8,128)} custom-call(s32[64]{0:T(128)} %table_ref.7, bf16[256,8192]{1,0:T(8,128)(2,1)} %act_ref.7, bf16[256,512]{1,0:T(8,128)(2,1)} %bitcast.15), custom_call_target="tpu_custom_call" | custom-call | flops 536870912 | bytes 8388608 | tf_op jit(solution)/shard_map/pallas_call | solution.py:62
  25.2 0.0 reduce-scatter.7.cloned.1.call-start
  25.2 8.5 %shard_map.77 = f32[8,2,512,128]{3,2,1,0:T(8,128)} custom-call(s32[64]{0:T(128)} %table_ref.7, bf16[256,8192]{1,0:T(8,128)(2,1)} %act_ref.7, bf16[256,512]{1,0:T(8,128)(2,1)} %bitcast.16), custom_call_target="tpu_custom_call" | custom-call | flops 536870912 | bytes 8388608 | tf_op jit(solution)/shard_map/pallas_call | solution.py:62
  33.8 0.0 reduce-scatter.5.cloned.1.call-start
  33.8 8.1 %shard_map.76 = f32[8,2,512,128]{3,2,1,0:T(8,128)} custom-call(s32[64]{0:T(128)} %table_ref.7, bf16[256,8192]{1,0:T(8,128)(2,1)} %act_ref.7, bf16[256,512]{1,0:T(8,128)(2,1)} %bitcast.17), custom_call_target="tpu_custom_call" | custom-call | flops 536870912 | bytes 8388608 | tf_op jit(solution)/shard_map/pallas_call | solution.py:62
  42.0 66.2 %reduce-scatter.11.cloned.1.call-done = f32[1,2,512,128]{3,2,1,0:T(8,128)} async-done(((f32[8,2,512,128]{3,2,1,0:T(8,128)}), f32[1,2,512,128]{3,2,1,0:T(8,128)}) %reduce-scatter.11.cloned.1.call-update) | async-done | bytes 524304 | tf_op jit(solution)/shard_map/reduce_scatter | solution.py:311
  108.1 24.5 %shard_map.80 = (f32[8,512,512]{2,1,0:T(8,128)}, f32[8,128,128]{2,1,0:T(8,128)}, bf16[2,512,128]{2,1,0:T(8,128)(2,1)}) custom-call(f32[2,512,128]{2,1,0:T(8,128)} %bitcast.31, f32[8,512,512]{2,1,0:T(8,128)} %bitcast.23, f32[8,128,128]{2,1,0:T(8,128)} %bitcast.27), custom_call_target="tpu_custom_call" | custom-call | flops 17179869184 | bytes 4194304 | tf_op jit(solution)/shard_map/pallas_call | solution.py:199
  132.6 67.1 %reduce-scatter.9.cloned.1.call-done = f32[1,2,512,128]{3,2,1,0:T(8,128)} async-done(((f32[8,2,512,128]{3,2,1,0:T(8,128)}), f32[1,2,512,128]{3,2,1,0:T(8,128)}) %reduce-scatter.9.cloned.1.call-update) | async-done | bytes 524304 | tf_op jit(solution)/shard_map/reduce_scatter | solution.py:311
  199.7 24.3 %shard_map.81 = (f32[8,512,512]{2,1,0:T(8,128)}, f32[8,128,128]{2,1,0:T(8,128)}, bf16[2,512,128]{2,1,0:T(8,128)(2,1)}) custom-call(f32[2,512,128]{2,1,0:T(8,128)} %bitcast.32, f32[8,512,512]{2,1,0:T(8,128)} %bitcast.24, f32[8,128,128]{2,1,0:T(8,128)} %bitcast.28, ...), custom_call_target="tpu_custom_call", output_to_operand_aliasing={{0}: (3, {}), {1}: (4, {})} | custom-call | flops 17179869184 | bytes 4194304 | tf_op jit(solution)/shard_map/pallas_call | solution.py:199
  224.0 67.3 %reduce-scatter.7.cloned.1.call-done = f32[1,2,512,128]{3,2,1,0:T(8,128)} async-done(((f32[8,2,512,128]{3,2,1,0:T(8,128)}), f32[1,2,512,128]{3,2,1,0:T(8,128)}) %reduce-scatter.7.cloned.1.call-update) | async-done | bytes 524304 | tf_op jit(solution)/shard_map/reduce_scatter | solution.py:311
  291.3 24.5 %shard_map.82 = (f32[8,512,512]{2,1,0:T(8,128)}, f32[8,128,128]{2,1,0:T(8,128)}, bf16[2,512,128]{2,1,0:T(8,128)(2,1)}) custom-call(f32[2,512,128]{2,1,0:T(8,128)} %bitcast.33, f32[8,512,512]{2,1,0:T(8,128)} %bitcast.25, f32[8,128,128]{2,1,0:T(8,128)} %bitcast.29, ...), custom_call_target="tpu_custom_call", output_to_operand_aliasing={{0}: (3, {}), {1}: (4, {})} | custom-call | flops 17179869184 | bytes 4194304 | tf_op jit(solution)/shard_map/pallas_call | solution.py:199
  315.8 67.5 %reduce-scatter.5.cloned.1.call-done = f32[1,2,512,128]{3,2,1,0:T(8,128)} async-done(((f32[8,2,512,128]{3,2,1,0:T(8,128)}), f32[1,2,512,128]{3,2,1,0:T(8,128)}) %reduce-scatter.5.cloned.1.call-update) | async-done | bytes 524304 | tf_op jit(solution)/shard_map/reduce_scatter | solution.py:311
  383.3 24.3 %shard_map.83 = (f32[8,512,512]{2,1,0:T(8,128)}, f32[8,128,128]{2,1,0:T(8,128)}, bf16[2,512,128]{2,1,0:T(8,128)(2,1)}) custom-call(f32[2,512,128]{2,1,0:T(8,128)} %bitcast.34, f32[8,512,512]{2,1,0:T(8,128)} %bitcast.26, f32[8,128,128]{2,1,0:T(8,128)} %bitcast.30, ...), custom_call_target="tpu_custom_call", output_to_operand_aliasing={{0}: (3, {}), {1}: (4, {})} | custom-call | flops 17179869184 | bytes 4194304 | tf_op jit(solution)/shard_map/pallas_call | solution.py:199
  407.7 0.5 all-gather.16.cloned.1.call-update
  408.3 0.7 all-gather.14.cloned.1.call-update
  409.1 0.7 all-gather.12.cloned.1.call-update
  409.8 0.1 add_multiply_fusion
  409.9 0.1 iota_add_fusion
  410.0 0.1 add.78
  410.1 0.2 select_reduce_fusion
  410.3 0.6 and_select_fusion
  410.9 45.7 %all-gather.18.cloned.1.call-done = bf16[16,512,128]{2,1,0:T(8,128)(2,1)} async-done(((bf16[2,512,128]{2,1,0:T(8,128)(2,1)}), bf16[16,512,128]{2,1,0:T(8,128)(2,1)}) %all-gather.18.cloned.1.call-update) | async-done | bytes 2097168 | tf_op jit(solution)/shard_map/all_gather | solution.py:317
  456.6 49.6 %all-gather.16.cloned.1.call-done = bf16[16,512,128]{2,1,0:T(8,128)(2,1)} async-done(((bf16[2,512,128]{2,1,0:T(8,128)(2,1)}), bf16[16,512,128]{2,1,0:T(8,128)(2,1)}) %all-gather.16.cloned.1.call-update) | async-done | bytes 2097168 | tf_op jit(solution)/shard_map/all_gather | solution.py:317
  506.2 49.8 %all-gather.14.cloned.1.call-done = bf16[16,512,128]{2,1,0:T(8,128)(2,1)} async-done(((bf16[2,512,128]{2,1,0:T(8,128)(2,1)}), bf16[16,512,128]{2,1,0:T(8,128)(2,1)}) %all-gather.14.cloned.1.call-update) | async-done | bytes 2097168 | tf_op jit(solution)/shard_map/all_gather | solution.py:317
  556.0 49.8 %all-gather.12.cloned.1.call-done = bf16[16,512,128]{2,1,0:T(8,128)(2,1)} async-done(((bf16[2,512,128]{2,1,0:T(8,128)(2,1)}), bf16[16,512,128]{2,1,0:T(8,128)(2,1)}) %all-gather.12.cloned.1.call-update) | async-done | bytes 2097168 | tf_op jit(solution)/shard_map/all_gather | solution.py:317
  605.8 0.6 rem.42.sub_ref
  606.3 3.0 shard_map.84
  609.4 33.7 %all-gather.10.cloned.1.call-done = bf16[2,1024,1024]{2,1,0:T(8,128)(2,1)} async-done(((bf16[2,1024,256]{2,1,0:T(8,128)(2,1)}), bf16[2,1024,1024]{2,1,0:T(8,128)(2,1)}) %all-gather.10.cloned.1.call-update) | async-done | bytes 4194320 | tf_op jit(solution)/shard_map/all_gather | solution.py:319
  643.1 4.6 copy.22
  (15 shorter events, 0.3 us)
Async XLA Ops:
  7.2 101.0 %reduce-scatter.11.cloned.1.call-start = ((), (), s32[]{:S(2)}) async-start(), calls=%async_computation.7 | async-start | bytes 4718592 | tf_op jit(solution)/shard_map/reduce_scatter | solution.py:311
  16.9 182.8 %reduce-scatter.9.cloned.1.call-start = ((), (), s32[]{:S(2)}) async-start(), calls=%async_computation.6 | async-start | bytes 4718592 | tf_op jit(solution)/shard_map/reduce_scatter | solution.py:311
  25.2 266.1 %reduce-scatter.7.cloned.1.call-start = ((), (), s32[]{:S(2)}) async-start(), calls=%async_computation.5 | async-start | bytes 4718592 | tf_op jit(solution)/shard_map/reduce_scatter | solution.py:311
  33.8 349.6 %reduce-scatter.5.cloned.1.call-start = ((), (), s32[]{:S(2)}) async-start(), calls=%async_computation.4 | async-start | bytes 4718592 | tf_op jit(solution)/shard_map/reduce_scatter | solution.py:311
  41.9 414.6 %all-gather.18.cloned.1.call-start = ((), (), s32[]{:S(2)}) async-start(), calls=%async_computation.12 | async-start | bytes 2359296 | tf_op jit(solution)/shard_map/all_gather | solution.py:317
  383.3 26.7 %copy-start = (s32[64]{0:T(128)S(1)}, s32[64]{0:T(128)}, u32[]{:S(2)}) copy-start(s32[64]{0:T(128)} %table_ref.7) | copy-start | bytes 772
  407.7 98.5 %all-gather.16.cloned.1.call-start = ((), (), s32[]{:S(2)}) async-start(), calls=%async_computation.11 | async-start | bytes 2359296 | tf_op jit(solution)/shard_map/all_gather | solution.py:317
  408.3 147.7 %all-gather.14.cloned.1.call-start = ((), (), s32[]{:S(2)}) async-start(), calls=%async_computation.10 | async-start | bytes 2359296 | tf_op jit(solution)/shard_map/all_gather | solution.py:317
  409.0 196.7 %all-gather.12.cloned.1.call-start = ((), (), s32[]{:S(2)}) async-start(), calls=%async_computation.9 | async-start | bytes 2359296 | tf_op jit(solution)/shard_map/all_gather | solution.py:317
  409.8 233.3 %all-gather.10.cloned.1.call-start = ((), (), s32[]{:S(2)}) async-start(), calls=%async_computation.8 | async-start | bytes 5242880 | tf_op jit(solution)/shard_map/all_gather | solution.py:319
Sparse Core Ops, SparseCore 0:
  17.1 91.0 reduce-scatter.10
  111.8 87.9 reduce-scatter.8
  203.4 87.8 reduce-scatter.6
  295.4 87.9 reduce-scatter.4
  407.8 48.7 all-gather.17
  458.6 47.6 all-gather.15
  508.3 47.6 all-gather.13
  558.1 47.6 all-gather.11
  609.5 33.5 all-gather.9
